TPU v7x, 32 devices: a whole 2x2x4 slice. The times are simulated.
32 devices in a mesh: face: 4 (over x, core), tile: 8 (over z, y).
Axes of the slice: x: 2, y: 2, z: 4, core: 2. Of those that a mesh axis runs over, the one named last changes fastest.
Arguments:
- field_in: bfloat16 [12, 48, 256, 256], P('face', None, 'tile'), may hold values from -6 to 6
- out_grad: bfloat16 [12, 48, 256, 256], P('face', None, 'tile'), may hold values from -6 to 6
- weight_first: bfloat16 [48, 48, 3, 3], replicated, may hold values from -0.3125 to 0.3125
- bias_first: float32 [48], replicated, may hold values from -3 to 3
- weight_second: bfloat16 [48, 48, 3, 3], replicated, may hold values from -0.3125 to 0.3125
- bias_second: float32 [48], replicated, may hold values from -3 to 3
- face_links: int32 [12, 4, 3], replicated, may hold values from 0 to 11, as said below
- corner_rules: int32 [12, 4], replicated, may hold values from 0 to 1
Outputs:
- output_field: bfloat16 [12, 48, 256, 256], P('face', None, 'tile')
- grad_field: bfloat16 [12, 48, 256, 256], P('face', None, 'tile')
- grad_weight_first: float32 [48, 48, 3, 3], replicated
- grad_bias_first: float32 [48], replicated
- grad_weight_second: float32 [48, 48, 3, 3], replicated
- grad_bias_second: float32 [48], replicated
Inputs may be any that keep to these rules, and one draw needn't show every extreme that they name: face_links[f, e] = (g, e2, r) glues edge e of face f to edge e2 of face g; r = 1 when positions along the two edges run in opposite directions. The gluing is a pairing: (g, e2) differs from (f, e) and face_links[g, e2] = (f, e, r). The partner face lies in 0..11, the edge in 0..3, the flag in 0..1.
All inputs are finite; a program needn't handle non-finite values.
Results may differ from a plain program's by a relative error of at most 0.0055.
The roundings to bfloat16 on the way count: a program that leaves them out, or rounds other values in their place, can miss the bound.
Values may be sent and summed in bfloat16 or wider, within the bound.
A program may use at most 256 MiB of HBM per device.

v0:
```python
import jax
import jax.numpy as jnp
from jax import lax
from jax.sharding import PartitionSpec as P

INV_ROOT_TWO = 0.7071067811865476
INV_ROOT_TWO_PI = 0.3989422804014327


def shortened(x):
    return jax.tree.map(lambda a: a.astype(jnp.bfloat16) if a.dtype == jnp.float32 else a, x)


def extended_2(block, sides, width):
    for axis, dim in sides:
        count = lax.axis_size(axis)
        forward = [(i, i + 1) for i in range(count - 1)]
        backward = [(target, source) for source, target in forward]
        low = lax.ppermute(
            lax.slice_in_dim(block, block.shape[dim] - width, None, axis=dim), axis, forward
        )
        high = lax.ppermute(lax.slice_in_dim(block, 0, width, axis=dim), axis, backward)
        block = jnp.concatenate([low, block, high], axis=dim)
    return block


def gelu_pair(values):
    normal_cdf = 0.5 * (1.0 + lax.erf(values * INV_ROOT_TWO))
    normal_pdf = jnp.exp(-0.5 * values * values) * INV_ROOT_TWO_PI
    return (values * normal_cdf, normal_cdf + values * normal_pdf)


def convolve(padded, weight):
    return lax.conv_general_dilated(
        padded,
        weight,
        (1, 1),
        "VALID",
        dimension_numbers=("NCHW", "OIHW", "NCHW"),
        preferred_element_type=jnp.float32,
    )


def halo_rows(strip):
    return extended_2(shortened(strip), (("tile", 2),), 1).astype(strip.dtype)


def place_lines(north_row, south_row, west_part, east_part, tile_pos, tile_count):
    seg_len = west_part.shape[-1]
    mirrored = tile_count - 1 - tile_pos
    blanks = jnp.zeros(north_row.shape, jnp.float32)
    north_full = jnp.where(tile_pos == 0, north_row.astype(jnp.float32), blanks)
    south_full = jnp.where(tile_pos == tile_count - 1, south_row.astype(jnp.float32), blanks)
    west_wide = west_part.astype(jnp.float32)
    east_wide = east_part.astype(jnp.float32)
    west_full = lax.dynamic_update_slice_in_dim(blanks, west_wide, tile_pos * seg_len, 2)
    east_full = lax.dynamic_update_slice_in_dim(blanks, east_wide, tile_pos * seg_len, 2)
    placed = jnp.stack([north_full, south_full, west_full, east_full], axis=1)
    own_lines = lax.psum(placed.astype(jnp.bfloat16), "tile")
    front = lax.dynamic_slice_in_dim(own_lines, tile_pos * seg_len, seg_len, 3)
    back = lax.dynamic_slice_in_dim(own_lines, mirrored * seg_len, seg_len, 3)
    return (front, back)


def partner_pieces(front, my_links, tile_pos, tile_count):
    faces_dev, _, channels, seg_len = front.shape
    side_len = seg_len * tile_count
    partner_face = my_links[:, :, 0].reshape(-1)
    partner_edge = my_links[:, :, 1].reshape(-1)
    flip_mask = (my_links[:, :, 2] == 1).reshape(-1)
    gathered = lax.all_gather(front, ("face", "tile"), axis=3, tiled=True)

    def fetch_line(face_id, edge_id):
        start = (face_id % faces_dev, edge_id, 0, face_id // faces_dev * side_len)
        return lax.dynamic_slice(gathered, start, (1, 1, channels, side_len))[0, 0]

    source = jax.vmap(fetch_line)(partner_face, partner_edge)
    ghosts = jnp.where(flip_mask[:, None, None], source[:, :, ::-1], source)
    ghosts = ghosts.reshape(faces_dev, 4, channels, side_len)
    north_row = ghosts[:, 0]
    south_row = ghosts[:, 1]
    west_part = lax.dynamic_slice_in_dim(ghosts[:, 2], tile_pos * seg_len, seg_len, 2)
    east_part = lax.dynamic_slice_in_dim(ghosts[:, 3], tile_pos * seg_len, seg_len, 2)
    return (north_row, south_row, west_part, east_part)


def fill_strip(activation, my_links, my_corners, tile_pos, tile_count):
    front, back = place_lines(
        activation[:, :, 0, :],
        activation[:, :, -1, :],
        activation[:, :, :, 0],
        activation[:, :, :, -1],
        tile_pos,
        tile_count,
    )
    north_row, south_row, west_part, east_part = partner_pieces(
        front, my_links, tile_pos, tile_count
    )
    corner_code = (my_corners == 0)[:, :, None]
    corner_nw = jnp.where(corner_code[:, 0], north_row[:, :, 0], west_part[:, :, 0])
    corner_ne = jnp.where(corner_code[:, 1], north_row[:, :, -1], east_part[:, :, 0])
    corner_sw = jnp.where(corner_code[:, 2], south_row[:, :, 0], west_part[:, :, -1])
    corner_se = jnp.where(corner_code[:, 3], south_row[:, :, -1], east_part[:, :, -1])
    middle = jnp.concatenate(
        [west_part[:, :, :, None], activation, east_part[:, :, :, None]], axis=3
    )
    extended = halo_rows(middle)
    top_row = jnp.concatenate([corner_nw[:, :, None], north_row, corner_ne[:, :, None]], axis=2)
    bottom_row = jnp.concatenate([corner_sw[:, :, None], south_row, corner_se[:, :, None]], axis=2)
    top_rim = jnp.where(tile_pos == 0, top_row, extended[:, :, 0])
    bottom_rim = jnp.where(tile_pos == tile_count - 1, bottom_row, extended[:, :, -1])
    return jnp.concatenate(
        [top_rim[:, :, None], extended[:, :, 1:-1], bottom_rim[:, :, None]], axis=2
    )


def unfold_strip(cotangent, weight, my_links, my_corners, tile_pos, tile_count):
    widened = jnp.pad(cotangent, ((0, 0), (0, 0), (0, 0), (1, 1)))
    extended = halo_rows(widened)
    padded = jnp.pad(extended, ((0, 0), (0, 0), (1, 1), (1, 1)))
    flipped = jnp.transpose(weight[:, :, ::-1, ::-1], (1, 0, 2, 3))
    pad_grad = convolve(padded, flipped)
    at_top = tile_pos == 0
    at_bottom = tile_pos == tile_count - 1
    north_row = pad_grad[:, :, 0, 1:-1]
    south_row = pad_grad[:, :, -1, 1:-1]
    west_part = pad_grad[:, :, 1:-1, 0]
    east_part = pad_grad[:, :, 1:-1, -1]
    corner_nw = pad_grad[:, :, 0, 0]
    corner_ne = pad_grad[:, :, 0, -1]
    corner_sw = pad_grad[:, :, -1, 0]
    corner_se = pad_grad[:, :, -1, -1]
    corner_code = my_corners[:, :, None]
    north_row = north_row.at[:, :, 0].add(jnp.where(corner_code[:, 0] == 0, corner_nw, 0.0))
    north_row = north_row.at[:, :, -1].add(jnp.where(corner_code[:, 1] == 0, corner_ne, 0.0))
    south_row = south_row.at[:, :, 0].add(jnp.where(corner_code[:, 2] == 0, corner_sw, 0.0))
    south_row = south_row.at[:, :, -1].add(jnp.where(corner_code[:, 3] == 0, corner_se, 0.0))
    west_part = west_part.at[:, :, 0].add(
        jnp.where((corner_code[:, 0] == 1) & at_top, corner_nw, 0.0)
    )
    west_part = west_part.at[:, :, -1].add(
        jnp.where((corner_code[:, 2] == 1) & at_bottom, corner_sw, 0.0)
    )
    east_part = east_part.at[:, :, 0].add(
        jnp.where((corner_code[:, 1] == 1) & at_top, corner_ne, 0.0)
    )
    east_part = east_part.at[:, :, -1].add(
        jnp.where((corner_code[:, 3] == 1) & at_bottom, corner_se, 0.0)
    )
    front, back = place_lines(
        north_row.astype(jnp.bfloat16),
        south_row.astype(jnp.bfloat16),
        west_part.astype(jnp.bfloat16),
        east_part.astype(jnp.bfloat16),
        tile_pos,
        tile_count,
    )
    back_north, back_south, back_west, back_east = partner_pieces(
        front, my_links, tile_pos, tile_count
    )
    interior = pad_grad[:, :, 1:-1, 1:-1]
    interior = interior.at[:, :, 0, :].add(jnp.where(at_top, back_north.astype(jnp.float32), 0.0))
    interior = interior.at[:, :, -1, :].add(
        jnp.where(at_bottom, back_south.astype(jnp.float32), 0.0)
    )
    interior = interior.at[:, :, :, 0].add(back_west.astype(jnp.float32))
    interior = interior.at[:, :, :, -1].add(back_east.astype(jnp.float32))
    return interior


def weight_grad(cotangent, padded):
    return lax.conv_general_dilated(
        padded,
        cotangent,
        (1, 1),
        "VALID",
        dimension_numbers=("CNHW", "IOHW", "CNHW"),
        preferred_element_type=jnp.float32,
    )


def body(
    field_in,
    out_grad,
    weight_first,
    bias_first,
    weight_second,
    bias_second,
    face_links,
    corner_rules,
):
    tile_count = lax.axis_size("tile")
    tile_pos = lax.axis_index("tile")
    face_pos = lax.axis_index("face")
    faces_dev = field_in.shape[0]
    side_len = field_in.shape[3]
    my_links = lax.dynamic_slice_in_dim(face_links, face_pos * faces_dev, faces_dev, 0)
    my_corners = lax.dynamic_slice_in_dim(corner_rules, face_pos * faces_dev, faces_dev, 0)
    padded_first = fill_strip(field_in, my_links, my_corners, tile_pos, tile_count)
    pre_first = convolve(padded_first, weight_first) + bias_first[None, :, None, None]
    gelu_first, slope_first = gelu_pair(pre_first)
    hidden = gelu_first.astype(jnp.bfloat16)
    padded_second = fill_strip(hidden, my_links, my_corners, tile_pos, tile_count)
    pre_second = convolve(padded_second, weight_second) + bias_second[None, :, None, None]
    gelu_second, slope_second = gelu_pair(pre_second)
    output_field = gelu_second.astype(jnp.bfloat16)
    grad_second = (out_grad.astype(jnp.float32) * slope_second).astype(jnp.bfloat16)
    weight_second_part = weight_grad(grad_second, padded_second)
    bias_second_part = jnp.sum(grad_second.astype(jnp.float32), axis=(0, 2, 3))
    grad_hidden = unfold_strip(
        grad_second, weight_second, my_links, my_corners, tile_pos, tile_count
    )
    grad_first = (grad_hidden * slope_first).astype(jnp.bfloat16)
    weight_first_part = weight_grad(grad_first, padded_first)
    bias_first_part = jnp.sum(grad_first.astype(jnp.float32), axis=(0, 2, 3))
    grad_field = unfold_strip(
        grad_first, weight_first, my_links, my_corners, tile_pos, tile_count
    ).astype(jnp.bfloat16)
    totals = lax.psum(
        (weight_first_part, bias_first_part, weight_second_part, bias_second_part), ("face", "tile")
    )
    return (
        output_field,
        grad_field,
        totals[0] / side_len,
        totals[1] / side_len,
        totals[2] / side_len,
        totals[3] / side_len,
    )


def solution(mesh):
    return jax.shard_map(
        body,
        mesh=mesh,
        in_specs=(
            P("face", None, "tile", None),
            P("face", None, "tile", None),
            P(),
            P(),
            P(),
            P(),
            P(),
            P(),
        ),
        out_specs=(
            P("face", None, "tile", None),
            P("face", None, "tile", None),
            P(),
            P(),
            P(),
            P(),
        ),
        check_vma=False,
    )
```

profile of v0, /device:TPU:0, one launch (start us, length us, event | category | flops | bytes accessed | tf_op | source)
XLA Modules:
  0.0 1963.4 jit_solution(1567796698921269111)
XLA Ops:
  19.2 74.5 %all-reduce.10.cloned.1.call-done = bf16[3,4,48,256]{3,2,0,1:T(8,128)(2,1)} async-done(((bf16[3,4,48,256]{3,2,0,1:T(8,128)(2,1)}), bf16[3,4,48,256]{3,2,0,1:T(8,128)(2,1)}) %all-reduce.10.cloned.1.call-update) | async-done | bytes 294928 | tf_op jit(solution)/shard_map/psum | solution.py:59
  103.9 51.9 %all-gather.5.cloned.1.call-done = bf16[3,4,48,1024]{2,1,0,3:T(4,128)(2,1)} async-done(((bf16[3,4,48,32]{2,1,0,3:T(4,128)(2,1)}), bf16[3,4,48,1024]{2,1,0,3:T(4,128)(2,1)}) %all-gather.5.cloned.1.call-update) | async-done | bytes 1179664 | tf_op jit(solution)/shard_map/all_gather | solution.py:71
  203.9 24.2 %copy.2867 = bf16[48,34,3,8,33]{4,3,0,2,1:T(8,128)(2,1)} copy(bf16[48,34,3,8,33]{0,2,4,3,1:T(4,128)(2,1)} %bitcast.324) | data formatting | bytes 5170176 | tf_op jit(solution)/shard_map/conv_general_dilated | solution.py:34
  268.8 23.4 %fusion.8 = (f32[32,24,33,48]{3,1,2,0:T(8,128)}, bf16[32,24,33,48]{3,1,2,0:T(8,128)(2,1)S(1)}) fusion(f32[48]{0:T(128)S(1)} %copy-done.49, pred[24,33]{0,1:T(8,128)(4,1)S(1)} %copy-done.53, bf16[48,48,3,3]{1,0,3,2:T(8,128)(2,1)S(1)} %copy-done.47, bf16[48,34,3,8,35]{0,3,2,4,1:T(8,128)(2,1)} %copy.2762), kind=kOutput, calls=%fused_computation.21 | convolution fusion | flops 1065664512 | bytes 10083288 | tf_op jit(solution)/shard_map/conv_general_dilated | solution.py:34
  311.7 72.1 %all-reduce.12.cloned.1.call-done = bf16[3,4,48,256]{3,2,0,1:T(8,128)(2,1)} async-done(((bf16[3,4,48,256]{3,2,0,1:T(8,128)(2,1)}), bf16[3,4,48,256]{3,2,0,1:T(8,128)(2,1)}) %all-reduce.12.cloned.1.call-update) | async-done | bytes 294928 | tf_op jit(solution)/shard_map/psum | solution.py:59
  386.0 59.4 %all-gather.7.cloned.1.call-done = bf16[3,4,48,1024]{2,1,0,3:T(4,128)(2,1)} async-done(((bf16[3,4,48,32]{2,1,0,3:T(4,128)(2,1)}), bf16[3,4,48,1024]{2,1,0,3:T(4,128)(2,1)}) %all-gather.7.cloned.1.call-update) | async-done | bytes 1179664 | tf_op jit(solution)/shard_map/all_gather | solution.py:71
  494.3 24.2 %copy.2872 = bf16[48,34,3,8,33]{4,3,0,2,1:T(8,128)(2,1)} copy(bf16[48,34,3,8,33]{0,2,4,3,1:T(4,128)(2,1)} %bitcast.325) | data formatting | bytes 5170176 | tf_op jit(solution)/shard_map/conv_general_dilated | solution.py:34
  559.2 22.5 %fusion.12 = (f32[32,24,33,48]{3,1,2,0:T(8,128)}, bf16[32,24,33,48]{3,1,2,0:T(8,128)(2,1)}) fusion(f32[48]{0:T(128)S(1)} %copy-done.50, pred[24,33]{0,1:T(8,128)(4,1)S(1)} %copy-done.53, bf16[48,48,3,3]{1,0,3,2:T(8,128)(2,1)S(1)} %copy-done, bf16[48,34,3,8,35]{0,3,2,4,1:T(8,128)(2,1)} %copy.2782), kind=kOutput, calls=%fused_computation.25 | convolution fusion | flops 1065664512 | bytes 10083288 | tf_op jit(solution)/shard_map/conv_general_dilated | solution.py:34
  694.7 22.0 %convolution_select_fusion.1 = f32[34,24,33,48]{3,1,2,0:T(8,128)} fusion(bf16[48,48,3,3]{1,0,3,2:T(8,128)(2,1)S(1)} %copy-done, bf16[48,34,3,8,35]{0,3,2,4,1:T(8,128)(2,1)} %copy.2790, pred[24,33]{0,1:T(8,128)(4,1)S(1)} %copy-done.51), kind=kOutput, calls=%fused_computation.37 | convolution fusion | flops 1096153344 | bytes 7954200 | tf_op jit(solution)/shard_map/conv_general_dilated | solution.py:34
  763.6 29.2 %fusion.67 = (f32[3,48,1,256]{2,1,0,3:T(8,128)}, f32[3,48,1,256]{2,1,0,3:T(8,128)}) fusion(f32[3,48,34,258]{2,1,0,3:T(8,128)} %bitcast.309), kind=kLoop, calls=%fused_computation.219 | loop fusion | bytes 589824 | tf_op jit(solution)/shard_map/slice | solution.py:125
  827.4 73.5 %all-reduce.14.cloned.1.call-done = bf16[3,4,48,256]{3,2,0,1:T(8,128)(2,1)} async-done(((bf16[3,4,48,256]{3,2,0,1:T(8,128)(2,1)}), bf16[3,4,48,256]{3,2,0,1:T(8,128)(2,1)}) %all-reduce.14.cloned.1.call-update) | async-done | bytes 294928 | tf_op jit(solution)/shard_map/psum | solution.py:59
  982.4 20.5 %slice_add_fusion.3 = f32[3,48,1,256]{2,1,0,3:T(8,128)} fusion(f32[3,48,1,256]{2,1,0,3:T(8,128)} %copy.2815, f32[3,48,34,258]{2,1,0,3:T(8,128)} %bitcast.315), kind=kLoop, calls=%fused_computation.14 | loop fusion | flops 36864 | bytes 442368 | tf_op jit(solution)/shard_map/add | solution.py:162
  1015.1 43.6 %scatter-add.94 = f32[3,48,32,256]{2,1,0,3:T(8,128)} dynamic-update-slice(f32[3,48,32,256]{2,1,0,3:T(8,128)} %slice.1002, f32[3,48,1,256]{2,1,0,3:T(8,128)} %slice_add_fusion.3, s32[]{:T(128)} %constant.616.clone.1, s32[]{:T(128)} %constant.616.clone.1, s32[]{:T(128)} %constant.616.clone.1, s32[]{:T(128)} %constant.616.clone.1) | dynamic-update-slice | bytes 294916 | tf_op jit(solution)/shard_map/scatter-add | solution.py:162
  1079.2 73.5 %scatter-add.95 = f32[3,48,32,256]{2,1,0,3:T(8,128)} dynamic-update-slice(f32[3,48,32,256]{2,1,0,3:T(8,128)} %scatter-add.94, f32[3,48,1,256]{2,1,0,3:T(8,128)} %slice_add_fusion.2, s32[]{:T(128)} %constant.616.clone.1, s32[]{:T(128)} %constant.616.clone.1, s32[]{:T(128)} %constant.635.clone.1, s32[]{:T(128)} %constant.616.clone.1) | dynamic-update-slice | bytes 294916 | tf_op jit(solution)/shard_map/scatter-add | solution.py:163
  1207.4 44.8 %fusion.75 = f32[48,48,3,3]{0,1,3,2:T(8,128)} fusion(bf16[3,48,32,256]{1,0,3,2:T(4,128)(2,1)} %copy.2858, bf16[3,48,1,258]{1,0,3,2:T(4,128)(2,1)S(1)} %copy-done.15, bf16[3,48,32,1]{1,0,3,2:T(4,128)(2,1)S(1)} %copy-done.23, bf16[3,48,32,256]{1,0,3,2:T(4,128)(2,1)} %bitcast.319, bf16[3,48,32,1]{1,0,3,2:T(4,128)(2,1)S(1)} %copy-done.21, ...), kind=kOutput, calls=%fused_computation.227 | convolution fusion | flops 1031847552 | bytes 4968576 | tf_op jit(solution)/shard_map/conv_general_dilated | solution.py:172
  1342.3 21.8 %convolution_select_fusion = f32[34,24,33,48]{3,1,2,0:T(8,128)} fusion(bf16[48,48,3,3]{1,0,3,2:T(8,128)(2,1)S(1)} %copy-done.48, bf16[48,34,3,8,35]{0,3,2,4,1:T(8,128)(2,1)} %copy.2828, pred[24,33]{0,1:T(8,128)(4,1)S(1)} %copy-done.52), kind=kOutput, calls=%fused_computation.36 | convolution fusion | flops 1096153344 | bytes 7954200 | tf_op jit(solution)/shard_map/conv_general_dilated | solution.py:34
  1411.0 29.3 %fusion.66 = (f32[3,48,1,256]{2,1,0,3:T(8,128)}, f32[3,48,1,256]{2,1,0,3:T(8,128)}) fusion(f32[3,48,34,258]{2,1,0,3:T(8,128)} %bitcast.302), kind=kLoop, calls=%fused_computation.218 | loop fusion | bytes 589824 | tf_op jit(solution)/shard_map/slice | solution.py:125
  1475.0 44.8 %fusion.74 = f32[48,48,3,3]{0,1,3,2:T(8,128)} fusion(bf16[3,48,32,256]{1,0,3,2:T(4,128)(2,1)} %copy.2857, bf16[3,48,1,258]{1,0,3,2:T(4,128)(2,1)S(1)} %copy-done.11, bf16[3,48,32,1]{1,0,3,2:T(4,128)(2,1)S(1)} %copy-done.19, bf16[3,48,32,256]{1,0,3,2:T(4,128)(2,1)} %copy.2758, bf16[3,48,32,1]{1,0,3,2:T(4,128)(2,1)S(1)} %copy-done.17, ...), kind=kOutput, calls=%fused_computation.226 | convolution fusion | flops 1031847552 | bytes 4968576 | tf_op jit(solution)/shard_map/conv_general_dilated | solution.py:172
  1520.1 28.0 %all-reduce.16.cloned.1.call-done = bf16[3,4,48,256]{3,2,0,1:T(8,128)(2,1)} async-done(((bf16[3,4,48,256]{3,2,0,1:T(8,128)(2,1)}), bf16[3,4,48,256]{3,2,0,1:T(8,128)(2,1)}) %all-reduce.16.cloned.1.call-update) | async-done | bytes 294928 | tf_op jit(solution)/shard_map/psum | solution.py:59
  1567.8 39.3 %all-reduce.2 = (f32[48]{0:T(128)S(1)}, f32[48]{0:T(128)S(1)}) all-reduce(f32[48]{0:T(128)S(1)} %copy-done.46, f32[48]{0:T(128)S(1)} %copy-done.45), channel_id=1, replica_groups=mesh['face'=4,'tile'=8] {'face','tile'}, use_global_device_ids=true, to_apply=%region_6.7 | all-reduce | flops 96 | bytes 768 | tf_op jit(solution)/shard_map/psum | solution.py:219
  1624.8 54.6 %all-reduce.18.cloned.1.call-done = (f32[48,48,3,3]{0,1,3,2:T(8,128)}, f32[48,48,3,3]{0,1,3,2:T(8,128)}) async-done(((f32[48,48,3,3]{0,1,3,2:T(8,128)}, f32[48,48,3,3]{0,1,3,2:T(8,128)}), (f32[48,48,3,3]{0,1,3,2:T(8,128)}, f32[48,48,3,3]{0,1,3,2:T(8,128)})) %all-reduce.18.cloned.1.call-update) | async-done | bytes 165904 | tf_op jit(solution)/shard_map/psum | solution.py:219
  1683.0 60.5 %all-gather.11.cloned.1.call-done = bf16[3,4,48,1024]{2,1,0,3:T(4,128)(2,1)} async-done(((bf16[3,4,48,32]{2,1,0,3:T(4,128)(2,1)}), bf16[3,4,48,1024]{2,1,0,3:T(4,128)(2,1)}) %all-gather.11.cloned.1.call-update) | async-done | bytes 1179664 | tf_op jit(solution)/shard_map/all_gather | solution.py:71
  1793.2 43.6 %scatter-add.114 = f32[3,48,32,256]{2,1,0,3:T(8,128)} dynamic-update-slice(f32[3,48,32,256]{2,1,0,3:T(8,128)} %slice.1030, f32[3,48,1,256]{2,1,0,3:T(8,128)} %slice_add_fusion.1, s32[]{:T(128)} %constant.616.clone.1, s32[]{:T(128)} %constant.616.clone.1, s32[]{:T(128)} %constant.616.clone.1, s32[]{:T(128)} %constant.616.clone.1) | dynamic-update-slice | bytes 294916 | tf_op jit(solution)/shard_map/scatter-add | solution.py:162
  1857.3 73.6 %scatter-add.115 = f32[3,48,32,256]{2,1,0,3:T(8,128)} dynamic-update-slice(f32[3,48,32,256]{2,1,0,3:T(8,128)} %scatter-add.114, f32[3,48,1,256]{2,1,0,3:T(8,128)} %slice_add_fusion, s32[]{:T(128)} %constant.616.clone.1, s32[]{:T(128)} %constant.616.clone.1, s32[]{:T(128)} %constant.635.clone.1, s32[]{:T(128)} %constant.616.clone.1) | dynamic-update-slice | bytes 294916 | tf_op jit(solution)/shard_map/scatter-add | solution.py:163
  (373 shorter events, 892.9 us)
Async XLA Ops:
  7.2 552.0 %copy-start = (bf16[48,48,3,3]{1,0,3,2:T(8,128)(2,1)S(1)}, bf16[48,48,3,3]{1,0,3,2:T(8,128)(2,1)}, u32[]{:S(2)}) copy-start(bf16[48,48,3,3]{1,0,3,2:T(8,128)(2,1)} %param.60) | copy-start | bytes 124420
  7.2 86.5 %all-reduce.10.cloned.1.call-start = ((), (), s32[]{:S(2)}) async-start(), calls=%async_computation | async-start | bytes 589824 | tf_op jit(solution)/shard_map/psum | solution.py:59
  19.2 136.6 %all-gather.5.cloned.1.call-start = ((), (), s32[]{:S(2)}) async-start(), calls=%async_computation.1 | async-start | bytes 3244032 | tf_op jit(solution)/shard_map/all_gather | solution.py:71
  95.5 288.3 %all-reduce.12.cloned.1.call-start = ((), (), s32[]{:S(2)}) async-start(), calls=%async_computation.2 | async-start | bytes 589824 | tf_op jit(solution)/shard_map/psum | solution.py:59
  103.4 345.7 %copy-start.25 = (pred[12]{0:T(512)(128)(4,1)}, pred[12]{0:T(512)(128)(4,1)S(1)}, u32[]{:S(2)}) copy-start(pred[12]{0:T(512)(128)(4,1)S(1)} %eq.133) | copy-start | bytes 40
  103.9 341.5 %copy-start.5 = (s32[12]{0:T(128)}, s32[12]{0:T(128)S(1)}, u32[]{:S(2)}) copy-start(s32[12]{0:T(128)S(1)} %fusion.63) | copy-start | bytes 148
  163.5 15.4 collective-permute-start
  167.1 12.0 collective-permute-start.1
  311.7 133.7 %all-gather.7.cloned.1.call-start = ((), (), s32[]{:S(2)}) async-start(), calls=%async_computation.3 | async-start | bytes 3244032 | tf_op jit(solution)/shard_map/all_gather | solution.py:71
  385.6 515.3 %all-reduce.14.cloned.1.call-start = ((), (), s32[]{:S(2)}) async-start(), calls=%async_computation.4 | async-start | bytes 589824 | tf_op jit(solution)/shard_map/psum | solution.py:59
  452.9 15.1 collective-permute-start.2
  456.3 12.0 collective-permute-start.3
  621.4 13.5 collective-permute-start.4
  625.8 9.1 collective-permute-start.5
  627.5 194.5 %copy-start.30 = (pred[3]{0:T(512)(128)(4,1)}, pred[3]{0:T(512)(128)(4,1)S(1)}, u32[]{:S(2)}) copy-start(pred[3]{0:T(512)(128)(4,1)S(1)} %get-tuple-element.456) | copy-start | bytes 13
  627.5 194.5 %copy-start.32 = (pred[3]{0:T(512)(128)(4,1)}, pred[3]{0:T(512)(128)(4,1)S(1)}, u32[]{:S(2)}) copy-start(pred[3]{0:T(512)(128)(4,1)S(1)} %get-tuple-element.457) | copy-start | bytes 13
  627.5 194.5 %copy-start.34 = (pred[3]{0:T(512)(128)(4,1)}, pred[3]{0:T(512)(128)(4,1)S(1)}, u32[]{:S(2)}) copy-start(pred[3]{0:T(512)(128)(4,1)S(1)} %get-tuple-element.460) | copy-start | bytes 13
  627.5 196.7 %copy-start.28 = (pred[3]{0:T(512)(128)(4,1)}, pred[3]{0:T(512)(128)(4,1)S(1)}, u32[]{:S(2)}) copy-start(pred[3]{0:T(512)(128)(4,1)S(1)} %get-tuple-element.459) | copy-start | bytes 13
  827.4 137.6 %all-gather.9.cloned.1.call-start = ((), (), s32[]{:S(2)}) async-start(), calls=%async_computation.5 | async-start | bytes 3244032 | tf_op jit(solution)/shard_map/all_gather | solution.py:71
  902.8 645.3 %all-reduce.16.cloned.1.call-start = ((), (), s32[]{:S(2)}) async-start(), calls=%async_computation.6 | async-start | bytes 589824 | tf_op jit(solution)/shard_map/psum | solution.py:59
  1191.2 90.2 %collective-permute-start.6 = (bf16[3,48,1,258]{3,1,2,0:T(8,128)(2,1)}, bf16[3,48,1,258]{3,1,2,0:T(8,128)(2,1)}, u32[]{:S(2)}, u32[]{:S(2)}) collective-permute-start(bf16[3,48,1,258]{3,1,2,0:T(8,128)(2,1)} %copy.2824), channel_id=1, source_target_pairs={{0,1},{1,2},{2,3},{3,4},{4,5},{5,6},{6,7},{8,9},{9,10},{10,11},{11... | collective-permute-start | bytes 222920 | tf_op jit(solution)/shard_map/ppermute | solution.py:19
  1206.1 75.3 %collective-permute-start.7 = (bf16[3,48,1,258]{3,1,2,0:T(8,128)(2,1)}, bf16[3,48,1,258]{3,1,2,0:T(8,128)(2,1)}, u32[]{:S(2)}, u32[]{:S(2)}) collective-permute-start(bf16[3,48,1,258]{3,1,2,0:T(8,128)(2,1)} %copy.2825), channel_id=1, source_target_pairs={{1,0},{2,1},{3,2},{4,3},{5,4},{6,5},{7,6},{9,8},{10,9},{11,10},{12... | collective-permute-start | bytes 222920 | tf_op jit(solution)/shard_map/ppermute | solution.py:22
  1474.9 204.5 %all-reduce.18.cloned.1.call-start = ((), (), s32[]{:S(2)}) async-start(), calls=%async_computation.8 | async-start | bytes 884736 | tf_op jit(solution)/shard_map/psum | solution.py:219
  1519.8 223.6 %all-gather.11.cloned.1.call-start = ((), (), s32[]{:S(2)}) async-start(), calls=%async_computation.7 | async-start | bytes 3244032 | tf_op jit(solution)/shard_map/all_gather | solution.py:71
  (47 other events, 2134.2 us)
Sparse Core Ops, SparseCore 0:
  19.3 74.3 all-reduce.9
  97.6 58.1 all-gather.4
  311.8 71.9 all-reduce.11
  387.2 58.1 all-gather.6
  827.5 73.4 all-reduce.13
  904.7 58.1 all-gather.8
  1475.0 72.9 all-reduce.15
  1554.0 125.3 all-reduce.17
  1683.3 60.0 all-gather.10
where the time goes:
time: 1990 us; the launch traced here: 1960 us
  local copies, waits for them, and re-layouts  973 us (49%)
  waiting for transfers between devices  499 us (25%)
  other arithmetic  236 us (12%)
  matrix products  179 us (9%)
  blocking collectives  39.3 us (2%)
  starting transfers between devices  21.1 us (1%)
    psum x4, waiting for transfers between devices, place_lines(): own_lines = lax.psum(placed.astype(jnp.bfloat16), 'tile')  248 us
    conv_general_dilated x16, local copies, waits for them, and re-layouts, convolve(): lax.conv_general_dilated(padded, weight, (1, 1), 'VALID', dimension_numbe...  238 us
    all_gather x4, waiting for transfers between devices, partner_pieces(): gathered = lax.all_gather(front, ('face', 'tile'), axis=3, tiled=True)  172 us
    scatter-add x2, local copies, waits for them, and re-layouts, unfold_strip(): interior.at[:, :, -1, :]  147 us
    unnamed x128, local copies, waits for them, and re-layouts  125 us
    conv_general_dilated x4, matrix products, convolve(): lax.conv_general_dilated(padded, weight, (1, 1), 'VALID', dimension_numbe...  89.7 us
    conv_general_dilated x2, matrix products, weight_grad(): lax.conv_general_dilated(padded, cotangent, (1, 1), 'VALID', dimension_nu...  89.7 us
    scatter-add x2, local copies, waits for them, and re-layouts, unfold_strip(): interior.at[:, :, 0, :]  87.2 us
  transfers between devices with their start and end apart: 17, of which 11 were waited for; matrix products, arithmetic and copies ran while one was open for 13% of the time, Pallas kernels for 0%

commit v1 on v0

--- a/solution.py
+++ b/solution.py
@@ -68,7 +68,22 @@
     partner_face = my_links[:, :, 0].reshape(-1)
     partner_edge = my_links[:, :, 1].reshape(-1)
     flip_mask = (my_links[:, :, 2] == 1).reshape(-1)
-    gathered = lax.all_gather(front, ("face", "tile"), axis=3, tiled=True)
+    ways, here, step = (
+        lax.axis_size(("face", "tile")),
+        lax.axis_index(("face", "tile")),
+        front.shape[3],
+    )
+    line, have = (front, 1)
+    while have < ways:
+        line = jnp.concatenate(
+            [
+                line,
+                lax.ppermute(line, ("face", "tile"), [(d, (d - have) % ways) for d in range(ways)]),
+            ],
+            axis=3,
+        )
+        have = 2 * have
+    gathered = jnp.roll(line, here * step, axis=3)
 
     def fetch_line(face_id, edge_id):
         start = (face_id % faces_dev, edge_id, 0, face_id // faces_dev * side_len)

time: 1990 us -> 2030 us (1.020)
  waiting for transfers between devices: 499 us -> 467 us
  local copies, waits for them, and re-layouts: 973 us -> 999 us
  starting transfers between devices: 21.1 us -> 44.4 us
  other arithmetic: 236 us -> 259 us
    all_gather x4 -> x0, waiting for transfers between devices: 172 us -> none  [partner_pieces(): gathered = lax.all_gather(front, ('face', 'tile'), axis=3, tiled=True)]
    ppermute x0 -> x20, waiting for transfers between devices: none -> 88.3 us  [partner_pieces(): lax.ppermute(line, ('face', 'tile'), [(d, (d - have) % ways) for d in ran...]
    psum x4, waiting for transfers between devices: 248 us -> 290 us  [place_lines(): own_lines = lax.psum(placed.astype(jnp.bfloat16), 'tile')]
    unnamed x128 -> x158, local copies, waits for them, and re-layouts: 125 us -> 144 us
  transfers between devices with their start and end apart: 17 -> 33, of which waited for: 11 -> 22; matrix products, arithmetic and copies ran while one was open for 13% -> 12% of each run, Pallas kernels for 0% -> 0%
where the time goes in v1:
time: 2030 us; the launch traced here: 2010 us
  local copies, waits for them, and re-layouts  999 us (49%)
  waiting for transfers between devices  467 us (23%)
  other arithmetic  259 us (13%)
  matrix products  180 us (9%)
  starting transfers between devices  44.4 us (2%)
  blocking collectives  39.9 us (2%)
    psum x4, waiting for transfers between devices, place_lines(): own_lines = lax.psum(placed.astype(jnp.bfloat16), 'tile')  290 us
    conv_general_dilated x16, local copies, waits for them, and re-layouts, convolve(): lax.conv_general_dilated(padded, weight, (1, 1), 'VALID', dimension_numbe...  238 us
    scatter-add x2, local copies, waits for them, and re-layouts, unfold_strip(): interior.at[:, :, -1, :]  147 us
    unnamed x158, local copies, waits for them, and re-layouts  144 us
    conv_general_dilated x4, matrix products, convolve(): lax.conv_general_dilated(padded, weight, (1, 1), 'VALID', dimension_numbe...  90.3 us
    conv_general_dilated x2, matrix products, weight_grad(): lax.conv_general_dilated(padded, cotangent, (1, 1), 'VALID', dimension_nu...  90.1 us
    ppermute x20, waiting for transfers between devices, partner_pieces(): lax.ppermute(line, ('face', 'tile'), [(d, (d - have) % ways) for d in ran...  88.3 us
    scatter-add x2, local copies, waits for them, and re-layouts, unfold_strip(): interior.at[:, :, 0, :]  87.2 us
  transfers between devices with their start and end apart: 33, of which 22 were waited for; matrix products, arithmetic and copies ran while one was open for 12% of the time, Pallas kernels for 0%

profile of v1, /device:TPU:0, one launch (start us, length us, event | category | flops | bytes accessed | tf_op | source)
XLA Modules:
  0.0 2005.1 jit_solution(7548753112284373707)
XLA Ops:
  19.2 74.5 %all-reduce.10.cloned.1.call-done = bf16[3,4,48,256]{3,2,1,0:T(8,128)(2,1)} async-done(((bf16[3,4,48,256]{3,2,1,0:T(8,128)(2,1)}), bf16[3,4,48,256]{3,2,1,0:T(8,128)(2,1)}) %all-reduce.10.cloned.1.call-update) | async-done | bytes 294928 | tf_op jit(solution)/shard_map/psum | solution.py:59
  201.0 24.2 %copy.2911 = bf16[48,34,3,8,33]{4,3,0,2,1:T(8,128)(2,1)} copy(bf16[48,34,3,8,33]{0,2,4,3,1:T(4,128)(2,1)} %bitcast.334) | data formatting | bytes 5170176 | tf_op jit(solution)/shard_map/conv_general_dilated | solution.py:34
  265.9 23.6 %fusion.8 = (f32[32,24,33,48]{3,1,2,0:T(8,128)}, bf16[32,24,33,48]{3,1,2,0:T(8,128)(2,1)S(1)}) fusion(f32[48]{0:T(128)S(1)} %copy-done.62, pred[24,33]{0,1:T(8,128)(4,1)S(1)} %copy-done.66, bf16[48,48,3,3]{1,0,3,2:T(8,128)(2,1)S(1)} %copy-done.60, bf16[48,34,3,8,35]{0,3,2,4,1:T(8,128)(2,1)} %copy.2804), kind=kOutput, calls=%fused_computation.21 | convolution fusion | flops 1065664512 | bytes 10083288 | tf_op jit(solution)/shard_map/conv_general_dilated | solution.py:34
  309.1 71.0 %all-reduce.12.cloned.1.call-done = bf16[3,4,48,256]{3,2,1,0:T(8,128)(2,1)} async-done(((bf16[3,4,48,256]{3,2,1,0:T(8,128)(2,1)}), bf16[3,4,48,256]{3,2,1,0:T(8,128)(2,1)}) %all-reduce.12.cloned.1.call-update) | async-done | bytes 294928 | tf_op jit(solution)/shard_map/psum | solution.py:59
  483.8 24.2 %copy.2920 = bf16[48,34,3,8,33]{4,3,0,2,1:T(8,128)(2,1)} copy(bf16[48,34,3,8,33]{0,2,4,3,1:T(4,128)(2,1)} %bitcast.335) | data formatting | bytes 5170176 | tf_op jit(solution)/shard_map/conv_general_dilated | solution.py:34
  548.7 22.5 %fusion.12 = (f32[32,24,33,48]{3,1,2,0:T(8,128)}, bf16[32,24,33,48]{3,1,2,0:T(8,128)(2,1)}) fusion(f32[48]{0:T(128)S(1)} %copy-done.63, pred[24,33]{0,1:T(8,128)(4,1)S(1)} %copy-done.66, bf16[48,48,3,3]{1,0,3,2:T(8,128)(2,1)S(1)} %copy-done, bf16[48,34,3,8,35]{0,3,2,4,1:T(8,128)(2,1)} %copy.2826), kind=kOutput, calls=%fused_computation.25 | convolution fusion | flops 1065664512 | bytes 10083288 | tf_op jit(solution)/shard_map/conv_general_dilated | solution.py:34
  683.6 22.2 %convolution_select_fusion.1 = f32[34,24,33,48]{3,1,2,0:T(8,128)} fusion(bf16[48,48,3,3]{1,0,3,2:T(8,128)(2,1)S(1)} %copy-done, bf16[48,34,3,8,35]{0,3,2,4,1:T(8,128)(2,1)} %copy.2834, pred[24,33]{0,1:T(8,128)(4,1)S(1)} %copy-done.64), kind=kOutput, calls=%fused_computation.37 | convolution fusion | flops 1096153344 | bytes 7954200 | tf_op jit(solution)/shard_map/conv_general_dilated | solution.py:34
  752.7 29.0 %fusion.71 = (f32[3,48,1,256]{2,1,0,3:T(8,128)}, f32[3,48,1,256]{2,1,0,3:T(8,128)}) fusion(f32[3,48,34,258]{2,1,0,3:T(8,128)} %bitcast.319), kind=kLoop, calls=%fused_computation.239 | loop fusion | bytes 589824 | tf_op jit(solution)/shard_map/slice | solution.py:140
  816.3 71.8 %all-reduce.14.cloned.1.call-done = bf16[3,4,48,256]{3,2,1,0:T(8,128)(2,1)} async-done(((bf16[3,4,48,256]{3,2,1,0:T(8,128)(2,1)}), bf16[3,4,48,256]{3,2,1,0:T(8,128)(2,1)}) %all-reduce.14.cloned.1.call-update) | async-done | bytes 294928 | tf_op jit(solution)/shard_map/psum | solution.py:59
  998.7 20.5 %slice_add_fusion.3 = f32[3,48,1,256]{2,1,0,3:T(8,128)} fusion(f32[3,48,1,256]{2,1,0,3:T(8,128)} %copy.2860, f32[3,48,34,258]{2,1,0,3:T(8,128)} %bitcast.325), kind=kLoop, calls=%fused_computation.14 | loop fusion | flops 36864 | bytes 442368 | tf_op jit(solution)/shard_map/add | solution.py:177
  1031.3 43.6 %scatter-add.94 = f32[3,48,32,256]{2,1,0,3:T(8,128)} dynamic-update-slice(f32[3,48,32,256]{2,1,0,3:T(8,128)} %slice.1002, f32[3,48,1,256]{2,1,0,3:T(8,128)} %slice_add_fusion.3, s32[]{:T(128)} %constant.634.clone.1, s32[]{:T(128)} %constant.634.clone.1, s32[]{:T(128)} %constant.634.clone.1, s32[]{:T(128)} %constant.634.clone.1) | dynamic-update-slice | bytes 294916 | tf_op jit(solution)/shard_map/scatter-add | solution.py:177
  1074.9 20.5 %slice_add_fusion.2 = f32[3,48,1,256]{2,1,0,3:T(8,128)} fusion(f32[3,48,1,256]{2,1,0,3:T(8,128)} %copy.2861, f32[3,48,32,256]{2,1,0,3:T(8,128)} %scatter-add.94), kind=kLoop, calls=%fused_computation.13 | loop fusion | flops 36864 | bytes 442368 | tf_op jit(solution)/shard_map/add | solution.py:178
  1095.4 73.6 %scatter-add.95 = f32[3,48,32,256]{2,1,0,3:T(8,128)} dynamic-update-slice(f32[3,48,32,256]{2,1,0,3:T(8,128)} %scatter-add.94, f32[3,48,1,256]{2,1,0,3:T(8,128)} %slice_add_fusion.2, s32[]{:T(128)} %constant.634.clone.1, s32[]{:T(128)} %constant.634.clone.1, s32[]{:T(128)} %constant.654.clone.1, s32[]{:T(128)} %constant.634.clone.1) | dynamic-update-slice | bytes 294916 | tf_op jit(solution)/shard_map/scatter-add | solution.py:178
  1298.3 22.0 %convolution_select_fusion = f32[34,24,33,48]{3,1,2,0:T(8,128)} fusion(bf16[48,48,3,3]{1,0,3,2:T(8,128)(2,1)S(1)} %copy-done.61, bf16[48,34,3,8,35]{0,3,2,4,1:T(8,128)(2,1)} %copy.2872, pred[24,33]{0,1:T(8,128)(4,1)S(1)} %copy-done.65), kind=kOutput, calls=%fused_computation.36 | convolution fusion | flops 1096153344 | bytes 7954200 | tf_op jit(solution)/shard_map/conv_general_dilated | solution.py:34
  1367.2 29.2 %fusion.70 = (f32[3,48,1,256]{2,1,0,3:T(8,128)}, f32[3,48,1,256]{2,1,0,3:T(8,128)}) fusion(f32[3,48,34,258]{2,1,0,3:T(8,128)} %bitcast.312), kind=kLoop, calls=%fused_computation.238 | loop fusion | bytes 589824 | tf_op jit(solution)/shard_map/slice | solution.py:140
  1435.1 72.9 %all-reduce.16.cloned.1.call-done = bf16[3,4,48,256]{3,2,1,0:T(8,128)(2,1)} async-done(((bf16[3,4,48,256]{3,2,1,0:T(8,128)(2,1)}), bf16[3,4,48,256]{3,2,1,0:T(8,128)(2,1)}) %all-reduce.16.cloned.1.call-update) | async-done | bytes 294928 | tf_op jit(solution)/shard_map/psum | solution.py:59
  1518.8 45.2 %fusion.79 = f32[48,48,3,3]{0,1,3,2:T(8,128)} fusion(bf16[3,48,32,256]{1,0,3,2:T(4,128)(2,1)} %copy.2902, bf16[3,48,1,258]{1,0,3,2:T(4,128)(2,1)S(1)} %copy-done.26, bf16[3,48,32,1]{1,0,3,2:T(4,128)(2,1)S(1)} %copy-done.34, bf16[3,48,32,256]{1,0,3,2:T(4,128)(2,1)} %bitcast.329, bf16[3,48,32,1]{1,0,3,2:T(4,128)(2,1)S(1)} %copy-done.32, ...), kind=kOutput, calls=%fused_computation.247 | convolution fusion | flops 1031847552 | bytes 4968576 | tf_op jit(solution)/shard_map/conv_general_dilated | solution.py:187
  1600.3 44.9 %fusion.78 = f32[48,48,3,3]{0,1,3,2:T(8,128)} fusion(bf16[3,48,32,256]{1,0,3,2:T(4,128)(2,1)} %copy.2901, bf16[3,48,1,258]{1,0,3,2:T(4,128)(2,1)S(1)} %copy-done.22, bf16[3,48,32,1]{1,0,3,2:T(4,128)(2,1)S(1)} %copy-done.30, bf16[3,48,32,256]{1,0,3,2:T(4,128)(2,1)} %copy.2800, bf16[3,48,32,1]{1,0,3,2:T(4,128)(2,1)S(1)} %copy-done.28, ...), kind=kOutput, calls=%fused_computation.246 | convolution fusion | flops 1031847552 | bytes 4968576 | tf_op jit(solution)/shard_map/conv_general_dilated | solution.py:187
  1645.2 39.9 %all-reduce.2 = (f32[48]{0:T(128)S(1)}, f32[48]{0:T(128)S(1)}) all-reduce(f32[48]{0:T(128)S(1)} %copy-done.59, f32[48]{0:T(128)S(1)} %copy-done.58), channel_id=1, replica_groups=mesh['face'=4,'tile'=8] {'face','tile'}, use_global_device_ids=true, to_apply=%region_6.8 | all-reduce | flops 96 | bytes 768 | tf_op jit(solution)/shard_map/psum | solution.py:234
  1706.3 64.0 %all-reduce.18.cloned.1.call-done = (f32[48,48,3,3]{0,1,3,2:T(8,128)}, f32[48,48,3,3]{0,1,3,2:T(8,128)}) async-done(((f32[48,48,3,3]{0,1,3,2:T(8,128)}, f32[48,48,3,3]{0,1,3,2:T(8,128)}), (f32[48,48,3,3]{0,1,3,2:T(8,128)}, f32[48,48,3,3]{0,1,3,2:T(8,128)})) %all-reduce.18.cloned.1.call-update) | async-done | bytes 165904 | tf_op jit(solution)/shard_map/psum | solution.py:234
  1802.5 20.5 %slice_add_fusion.1 = f32[3,48,1,256]{2,1,0,3:T(8,128)} fusion(f32[3,48,1,256]{2,1,0,3:T(8,128)} %copy.2897, f32[3,48,34,258]{2,1,0,3:T(8,128)} %bitcast.318), kind=kLoop, calls=%fused_computation.12 | loop fusion | flops 36864 | bytes 442368 | tf_op jit(solution)/shard_map/add | solution.py:177
  1835.0 43.6 %scatter-add.114 = f32[3,48,32,256]{2,1,0,3:T(8,128)} dynamic-update-slice(f32[3,48,32,256]{2,1,0,3:T(8,128)} %slice.1030, f32[3,48,1,256]{2,1,0,3:T(8,128)} %slice_add_fusion.1, s32[]{:T(128)} %constant.634.clone.1, s32[]{:T(128)} %constant.634.clone.1, s32[]{:T(128)} %constant.634.clone.1, s32[]{:T(128)} %constant.634.clone.1) | dynamic-update-slice | bytes 294916 | tf_op jit(solution)/shard_map/scatter-add | solution.py:177
  1878.6 20.5 %slice_add_fusion = f32[3,48,1,256]{2,1,0,3:T(8,128)} fusion(f32[3,48,1,256]{2,1,0,3:T(8,128)} %copy.2898, f32[3,48,32,256]{2,1,0,3:T(8,128)} %scatter-add.114), kind=kLoop, calls=%fused_computation.11 | loop fusion | flops 36864 | bytes 442368 | tf_op jit(solution)/shard_map/add | solution.py:178
  1899.0 73.5 %scatter-add.115 = f32[3,48,32,256]{2,1,0,3:T(8,128)} dynamic-update-slice(f32[3,48,32,256]{2,1,0,3:T(8,128)} %scatter-add.114, f32[3,48,1,256]{2,1,0,3:T(8,128)} %slice_add_fusion, s32[]{:T(128)} %constant.634.clone.1, s32[]{:T(128)} %constant.634.clone.1, s32[]{:T(128)} %constant.654.clone.1, s32[]{:T(128)} %constant.634.clone.1) | dynamic-update-slice | bytes 294916 | tf_op jit(solution)/shard_map/scatter-add | solution.py:178
  (451 shorter events, 992.2 us)
Async XLA Ops:
  7.2 86.5 %all-reduce.10.cloned.1.call-start = ((), (), s32[]{:S(2)}) async-start(), calls=%async_computation | async-start | bytes 589824 | tf_op jit(solution)/shard_map/psum | solution.py:59
  19.2 360.9 %all-reduce.12.cloned.1.call-start = ((), (), s32[]{:S(2)}) async-start(), calls=%async_computation.1 | async-start | bytes 589824 | tf_op jit(solution)/shard_map/psum | solution.py:59
  106.1 9.1 collective-permute-start.2
  121.9 15.8 collective-permute-start.4
  156.6 18.0 collective-permute-start.5
  163.1 11.8 collective-permute-start.6
  309.0 579.0 %all-reduce.14.cloned.1.call-start = ((), (), s32[]{:S(2)}) async-start(), calls=%async_computation.2 | async-start | bytes 589824 | tf_op jit(solution)/shard_map/psum | solution.py:59
  392.4 9.1 collective-permute-start.9
  406.6 15.4 collective-permute-start.11
  439.2 18.1 collective-permute-start.12
  445.7 11.9 collective-permute-start.13
  610.4 13.4 collective-permute-start.14
  614.8 9.0 collective-permute-start.15
  816.2 691.8 %all-reduce.16.cloned.1.call-start = ((), (), s32[]{:S(2)}) async-start(), calls=%async_computation.3 | async-start | bytes 589824 | tf_op jit(solution)/shard_map/psum | solution.py:59
  900.4 9.1 collective-permute-start.18
  914.4 56.6 %collective-permute-start.20 = (bf16[3,4,48,512]{3,2,1,0:T(8,128)(2,1)S(1)}, bf16[3,4,48,512]{3,2,1,0:T(8,128)(2,1)S(1)}, u32[]{:S(2)}, u32[]{:S(2)}) collective-permute-start(bf16[3,4,48,512]{3,2,1,0:T(8,128)(2,1)S(1)} %concatenate.226), channel_id=1, source_target_pairs={{0,16},{1,17},{2,18},{3,19},{4,20},{5,21},{6,22},{7,23},{8,24},{9,... | collective-permute-start | bytes 1769480 | tf_op jit(solution)/shard_map/ppermute | solution.py:81
  1206.1 32.4 %collective-permute-start.21 = (bf16[3,48,1,258]{3,1,2,0:T(8,128)(2,1)S(1)}, bf16[3,48,1,258]{3,1,2,0:T(8,128)(2,1)S(1)}, u32[]{:S(2)}, u32[]{:S(2)}) collective-permute-start(bf16[3,48,1,258]{3,1,2,0:T(8,128)(2,1)S(1)} %copy.2868), channel_id=1, source_target_pairs={{0,1},{1,2},{2,3},{3,4},{4,5},{5,6},{6,7},{8,9},{9,10},{10,11},{11... | collective-permute-start | bytes 222920 | tf_op jit(solution)/shard_map/ppermute | solution.py:19
  1223.0 15.5 collective-permute-start.22
  1435.0 335.3 %all-reduce.18.cloned.1.call-start = ((), (), s32[]{:S(2)}) async-start(), calls=%async_computation.4 | async-start | bytes 884736 | tf_op jit(solution)/shard_map/psum | solution.py:234
  1509.0 7.8 collective-permute-start.23
  1517.6 47.6 %collective-permute-start.24 = (bf16[3,4,48,64]{3,2,1,0:T(8,128)(2,1)}, bf16[3,4,48,64]{3,2,1,0:T(8,128)(2,1)}, u32[]{:S(2)}, u32[]{:S(2)}) collective-permute-start(bf16[3,4,48,64]{3,2,1,0:T(8,128)(2,1)} %pad_maximum_fusion.22), channel_id=1, source_target_pairs={{0,30},{1,31},{2,0},{3,1},{4,2},{5,3},{6,4},{7,5},{8,6},{9,7},{10,... | collective-permute-start | bytes 221192 | tf_op jit(solution)/shard_map/ppermute | solution.py:81
  1566.3 29.1 %collective-permute-start.25 = (bf16[3,4,48,128]{3,2,1,0:T(8,128)(2,1)S(1)}, bf16[3,4,48,128]{3,2,1,0:T(8,128)(2,1)S(1)}, u32[]{:S(2)}, u32[]{:S(2)}) collective-permute-start(bf16[3,4,48,128]{3,2,1,0:T(8,128)(2,1)S(1)} %pad_maximum_fusion.23), channel_id=1, source_target_pairs={{0,28},{1,29},{2,30},{3,31},{4,0},{5,1},{6,2},{7,3},{8,4},{9,5},{1... | collective-permute-start | bytes 442376 | tf_op jit(solution)/shard_map/ppermute | solution.py:81
  1597.3 88.3 %collective-permute-start.26 = (bf16[3,4,48,256]{3,2,1,0:T(8,128)(2,1)}, bf16[3,4,48,256]{3,2,1,0:T(8,128)(2,1)}, u32[]{:S(2)}, u32[]{:S(2)}) collective-permute-start(bf16[3,4,48,256]{3,2,1,0:T(8,128)(2,1)} %pad_maximum_fusion.9), channel_id=1, source_target_pairs={{0,24},{1,25},{2,26},{3,27},{4,28},{5,29},{6,30},{7,31},{8,0},{9,1... | collective-permute-start | bytes 884744 | tf_op jit(solution)/shard_map/ppermute | solution.py:81
  1687.0 86.9 %collective-permute-start.27 = (bf16[3,4,48,512]{3,2,1,0:T(8,128)(2,1)S(1)}, bf16[3,4,48,512]{3,2,1,0:T(8,128)(2,1)S(1)}, u32[]{:S(2)}, u32[]{:S(2)}) collective-permute-start(bf16[3,4,48,512]{3,2,1,0:T(8,128)(2,1)S(1)} %concatenate.232), channel_id=1, source_target_pairs={{0,16},{1,17},{2,18},{3,19},{4,20},{5,21},{6,22},{7,23},{8,24},{9,... | collective-permute-start | bytes 1769480 | tf_op jit(solution)/shard_map/ppermute | solution.py:81
  (76 other events, 4948.6 us)
Sparse Core Ops, SparseCore 0:
  19.3 74.3 all-reduce.9
  309.1 70.8 all-reduce.11
  816.3 71.6 all-reduce.13
  1435.1 72.7 all-reduce.15
  1645.3 124.9 all-reduce.17
